TPU v7x, 32 devices: a whole 2x2x4 slice. The times are simulated.
32 devices in a mesh: frame: 8 (over z, y), height: 4 (over x, core).
Axes of the slice: x: 2, y: 2, z: 4, core: 2. Of those that a mesh axis runs over, the one named last changes fastest.
Arguments:
- latents: bfloat16 [8, 24, 64, 1152], P('frame', 'height'), may hold values from -30 to 30
- qkv_weight: bfloat16 [2, 1152, 1728], replicated, as said below
- out_weight: bfloat16 [2, 576, 1152], replicated, may hold values from -0.25 to 0.25
Outputs:
- result: bfloat16 [8, 24, 64, 1152], P('frame', 'height')
Inputs may be any that keep to these rules, and one draw needn't show every extreme that they name: `qkv_weight`: entries lie within -0.2 to 0.2.
All inputs are finite; a program needn't handle non-finite values.
Results may differ from a plain program's by a relative error of at most 0.0095.
Values may be sent and summed in bfloat16 or wider, within the bound.
No kernel may reach another device: no remote copies, remote signals or barrier semaphores. Data moves between devices by JAX's collectives and lax.ppermute only.
A program may use at most 64 MiB of HBM per device.

v0:
```python
import jax
import jax.numpy as jnp
from jax import lax
from jax.sharding import PartitionSpec as P

HEAD_DIM = 72


def layer_norm(values):
    values = values.astype(jnp.float32)
    center = values - jnp.mean(values, axis=-1, keepdims=True)
    spread = jnp.mean(center * center, axis=-1, keepdims=True)
    return (center * lax.rsqrt(spread + 1e-06)).astype(jnp.bfloat16)


def project(tokens, weight):
    normed = layer_norm(tokens)
    flattened = normed.reshape(-1, normed.shape[-1])
    joined = jnp.dot(flattened, weight, preferred_element_type=jnp.float32)
    return joined.astype(jnp.bfloat16).reshape(tokens.shape[:-1] + (weight.shape[1],))


def attend(joined):
    length, batches = (joined.shape[0], joined.shape[1])
    inner_width = joined.shape[2] // 3
    head_count = inner_width // HEAD_DIM
    query_rows = joined[:, :, :inner_width].reshape(length, batches, head_count, HEAD_DIM)
    key_rows = joined[:, :, inner_width : 2 * inner_width].reshape(
        length, batches, head_count, HEAD_DIM
    )
    value_rows = joined[:, :, 2 * inner_width :].reshape(length, batches, head_count, HEAD_DIM)
    scores = jnp.einsum(
        "lbnd,mbnd->bnlm", query_rows, key_rows, preferred_element_type=jnp.float32
    ) * HEAD_DIM ** (-0.5)
    scores = scores - jnp.max(scores, axis=-1, keepdims=True)
    exponent = jnp.exp(scores)
    weights = (exponent / jnp.sum(exponent, axis=-1, keepdims=True)).astype(jnp.bfloat16)
    mixture = jnp.einsum("bnlm,mbnd->lbnd", weights, value_rows, preferred_element_type=jnp.float32)
    return mixture.reshape(length, batches, inner_width).astype(jnp.bfloat16)


def residual(tokens, mixture, weight):
    update = jnp.dot(
        mixture.reshape(-1, mixture.shape[-1]), weight, preferred_element_type=jnp.float32
    )
    return (tokens.astype(jnp.float32) + update.reshape(tokens.shape)).astype(jnp.bfloat16)


def frames_block(joined):
    length, single, places, triple = joined.shape
    mixture = attend(joined.reshape(length, single * places, triple))
    return mixture.reshape(length, single, places, triple // 3)


def per_device(latents, qkv_weight, out_weight):
    frames_dev, rows_dev, columns, feature_width = latents.shape
    frame_count = lax.axis_size("frame")
    rows_attend = jax.vmap(attend)
    rows_att = rows_attend(
        project(
            lax.all_to_all(latents, "height", split_axis=2, concat_axis=1, tiled=True),
            qkv_weight[0],
        )
    )
    rows_att = lax.all_to_all(rows_att, "height", split_axis=1, concat_axis=2, tiled=True)
    middle = residual(latents, rows_att, out_weight[0])
    places_dev = rows_dev * columns // frame_count
    grouped = middle.reshape(frames_dev, frame_count, places_dev, feature_width)
    frames_att = frames_block(
        project(
            lax.all_to_all(grouped, "frame", split_axis=1, concat_axis=0, tiled=True), qkv_weight[1]
        )
    )
    frames_att = lax.all_to_all(frames_att, "frame", split_axis=0, concat_axis=1, tiled=True)
    frames_att = frames_att.reshape(frames_dev, rows_dev, columns, frames_att.shape[-1])
    return residual(middle, frames_att, out_weight[1])


def solution(mesh):
    return jax.shard_map(
        per_device,
        mesh=mesh,
        in_specs=(P("frame", "height", None, None), P(), P()),
        out_specs=P("frame", "height", None, None),
        check_vma=False,
    )
```

profile of v0, /device:TPU:0, one launch (start us, length us, event | category | flops | bytes accessed | tf_op | source)
XLA Modules:
  0.0 113.4 jit_solution(6258203247795227640)
XLA Ops:
  0.0 1.7 %copy.33 = bf16[1,6,64,1152]{3,1,0,2:T(8,128)(2,1)S(1)} copy(bf16[1,6,64,1152]{3,2,1,0:T(8,128)(2,1)} %param.3) | data formatting | bytes 1769472 | tf_op args[0]
  1.7 20.1 %all_to_all.42 = bf16[1,6,64,1152]{3,1,0,2:T(8,128)(2,1)S(1)} all-to-all(bf16[1,6,64,1152]{3,1,0,2:T(8,128)(2,1)S(1)} %copy.33), channel_id=1, replica_groups=mesh['frame'=8,'height'=4] {'height'}, dimensions={2} | all-to-all | bytes 1769472 | tf_op jit(solution)/shard_map/all_to_all | solution.py:61
  21.9 0.2 fusion.24
  22.2 0.4 fusion.27
  22.5 0.3 fusion.28
  22.9 2.4 %fusion.12 = bf16[384,1728]{0,1:T(8,128)(2,1)S(1)} fusion(bf16[384,1152]{1,0:T(8,128)(2,1)S(1)} %bitcast.98, bf16[2,1152,1728]{1,2,0:T(8,128)(2,1)S(1)} %copy-done.5), kind=kOutput, calls=%fused_computation.14 | convolution fusion | flops 1529487360 | bytes 6193152 | tf_op jit(solution)/shard_map/dot_general | solution.py:19
  25.3 1.8 %copy.36 = bf16[384,1728]{1,0:T(8,128)(2,1)S(1)} copy(bf16[384,1728]{0,1:T(8,128)(2,1)S(1)} %fusion.12) | data formatting | bytes 2654208 | tf_op jit(solution)/shard_map/convert_element_type | solution.py:20
  27.1 0.3 fusion.68
  27.3 0.8 reshape.264
  28.1 0.8 reshape.265
  28.9 1.7 %reshape.263 = bf16[24,16,8,72]{3,2,1,0:T(8,128)(2,1)} reshape(bf16[1,24,16,576]{3,2,1,0:T(8,128)(2,1)S(1)} %get-tuple-element.8) | data formatting | bytes 884736 | tf_op jit(solution)/shard_map/reshape.7
  30.6 2.6 %fusion.69 = (f32[16,8,24]{2,1,0:T(8,128)S(1)}, f32[16,8,24,24]{2,3,1,0:T(8,128)}) fusion(bf16[24,16,8,72]{3,2,1,0:T(8,128)(2,1)S(1)} %reshape.265, bf16[24,16,8,72]{3,2,1,0:T(8,128)(2,1)S(1)} %reshape.264), kind=kOutput, calls=%fused_computation.65 | convolution fusion | flops 10838039 | bytes 1191936 | tf_op jit(solution)/shard_map/vmap()/sub | solution.py:35
  33.2 2.1 %fusion.37 = bf16[1,24,16,8,72]{4,1,3,2,0:T(8,128)(2,1)S(1)} fusion(f32[16,8,24,24]{2,3,1,0:T(8,128)} %get-tuple-element.12, bf16[24,16,8,72]{3,2,1,0:T(8,128)(2,1)S(1)} %copy-done.3, f32[16,8,24]{2,1,0:T(8,128)S(1)} %get-tuple-element.11), kind=kOutput, calls=%fused_computation.45 | convolution fusion | flops 10985472 | bytes 1191936 | tf_op jit(solution)/shard_map/vmap(bnlm,mbnd->lbnd)/dot_general | solution.py:38
  35.4 0.2 copy.41
  35.5 0.6 convert_element_type.136
  36.1 10.9 %all_to_all.43 = bf16[1,24,16,576]{3,2,0,1:T(8,128)(2,1)S(1)} all-to-all(bf16[1,24,16,576]{3,2,0,1:T(8,128)(2,1)S(1)} %bitcast.93), channel_id=1, replica_groups=mesh['frame'=8,'height'=4] {'height'}, dimensions={1} | all-to-all | bytes 884736 | tf_op jit(solution)/shard_map/all_to_all | solution.py:65
  47.0 2.3 %fusion.10 = bf16[1,6,64,1152]{3,2,1,0:T(8,128)(2,1)S(1)} fusion(bf16[6,64,576]{2,1,0:T(8,128)(2,1)S(1)} %bitcast.100, bf16[1,6,64,1152]{3,2,1,0:T(8,128)(2,1)S(1)} %copy-done.2, bf16[2,576,1152]{2,1,0:T(8,128)(2,1)} %param.5), kind=kOutput, calls=%fused_computation.12 | convolution fusion | flops 510935040 | bytes 3538944 | tf_op jit(solution)/shard_map/dot_general | solution.py:43
  49.3 28.1 %all_to_all.44 = bf16[1,8,48,1152]{3,2,0,1:T(8,128)(2,1)S(1)} all-to-all(bf16[1,8,48,1152]{3,2,0,1:T(8,128)(2,1)S(1)} %bitcast.96), channel_id=1, replica_groups=mesh['frame'=8,'height'=4] {'frame'}, dimensions={1} | all-to-all | bytes 1769472 | tf_op jit(solution)/shard_map/all_to_all | solution.py:71
  77.5 0.2 convert_reduce_fusion
  77.7 0.4 fusion.22
  78.1 0.3 fusion.19
  78.4 4.5 %fusion.15 = bf16[384,1728]{0,1:T(8,128)(2,1)S(1)} fusion(bf16[384,1152]{1,0:T(8,128)(2,1)S(1)} %bitcast.97, bf16[2,1152,1728]{1,2,0:T(8,128)(2,1)} %param.4), kind=kOutput, calls=%fused_computation.15 | convolution fusion | flops 1529487360 | bytes 6193152 | tf_op jit(solution)/shard_map/dot_general | solution.py:19
  82.8 1.8 %copy.45 = bf16[384,1728]{1,0:T(8,128)(2,1)S(1)} copy(bf16[384,1728]{0,1:T(8,128)(2,1)S(1)} %fusion.15) | data formatting | bytes 2654208 | tf_op jit(solution)/shard_map/convert_element_type | solution.py:20
  84.6 0.3 fusion.67
  84.9 0.8 reshape.269
  85.7 0.8 reshape.270
  86.5 1.7 %reshape.268 = bf16[8,48,8,72]{3,2,1,0:T(8,128)(2,1)} reshape(bf16[8,48,576]{2,1,0:T(8,128)(2,1)S(1)} %get-tuple-element.5) | data formatting | bytes 884736 | tf_op jit(solution)/shard_map/reshape | solution.py:31
  88.1 2.8 %fusion.74 = (f32[48,8,8]{2,1,0:T(8,128)S(1)}, f32[48,8,8,8]{2,3,1,0:T(8,128)}) fusion(bf16[8,48,8,72]{3,2,1,0:T(8,128)(2,1)S(1)} %reshape.270, bf16[8,48,8,72]{3,2,1,0:T(8,128)(2,1)S(1)} %reshape.269), kind=kOutput, calls=%fused_computation.66 | convolution fusion | flops 3612679 | bytes 995328 | tf_op jit(solution)/shard_map/sub | solution.py:35
  90.9 2.2 %fusion.38 = bf16[8,48,8,72]{3,0,2,1:T(8,128)(2,1)S(1)} fusion(f32[48,8,8,8]{2,3,1,0:T(8,128)} %get-tuple-element.14, bf16[8,48,8,72]{3,2,1,0:T(8,128)(2,1)S(1)} %copy-done.4, f32[48,8,8]{2,1,0:T(8,128)S(1)} %get-tuple-element.13), kind=kOutput, calls=%fused_computation.46 | convolution fusion | flops 3809280 | bytes 995328 | tf_op jit(solution)/shard_map/bnlm,mbnd->lbnd/dot_general | solution.py:38
  93.2 0.6 convert_element_type.147
  93.8 16.4 %all_to_all.45 = bf16[8,1,48,576]{3,2,1,0:T(8,128)(2,1)S(1)} all-to-all(bf16[8,1,48,576]{3,2,1,0:T(8,128)(2,1)S(1)} %bitcast.95), channel_id=1, replica_groups=mesh['frame'=8,'height'=4] {'frame'}, dimensions={0} | all-to-all | bytes 884736 | tf_op jit(solution)/shard_map/all_to_all | solution.py:74
  110.2 3.2 %fusion.11 = bf16[1,6,64,1152]{3,2,1,0:T(8,128)(2,1)} fusion(bf16[6,64,576]{2,1,0:T(8,128)(2,1)S(1)} %bitcast.99, bf16[1,6,64,1152]{3,2,1,0:T(8,128)(2,1)S(1)} %copy-done.1, bf16[2,576,1152]{2,1,0:T(8,128)(2,1)} %param.5), kind=kOutput, calls=%fused_computation.13 | convolution fusion | flops 510935040 | bytes 3538944 | tf_op jit(solution)/shard_map/dot_general | solution.py:43
  (20 shorter events, 0.4 us)
Async XLA Ops:
  1.7 21.2 %copy-start.5 = (bf16[2,1152,1728]{1,2,0:T(8,128)(2,1)S(1)}, bf16[2,1152,1728]{1,2,0:T(8,128)(2,1)}, u32[]{:S(2)}) copy-start(bf16[2,1152,1728]{1,2,0:T(8,128)(2,1)} %param.4) | copy-start | bytes 23887876
  30.6 2.6 %copy-start.3 = (bf16[24,16,8,72]{3,2,1,0:T(8,128)(2,1)S(1)}, bf16[24,16,8,72]{3,2,1,0:T(8,128)(2,1)}, u32[]{:S(2)}) copy-start(bf16[24,16,8,72]{3,2,1,0:T(8,128)(2,1)} %reshape.263) | copy-start | bytes 1327108
  35.5 11.5 %copy-start.2 = (bf16[1,6,64,1152]{3,2,1,0:T(8,128)(2,1)S(1)}, bf16[1,6,64,1152]{3,2,1,0:T(8,128)(2,1)}, u32[]{:S(2)}) copy-start(bf16[1,6,64,1152]{3,2,1,0:T(8,128)(2,1)} %param.3) | copy-start | bytes 2654212
  49.3 28.7 %copy-start = (bf16[1,6,64,1152]{3,2,1,0:T(8,128)(2,1)}, bf16[1,6,64,1152]{3,2,1,0:T(8,128)(2,1)S(1)}, u32[]{:S(2)}) copy-start(bf16[1,6,64,1152]{3,2,1,0:T(8,128)(2,1)S(1)} %fusion.10) | copy-start | bytes 2654212
  88.1 2.8 %copy-start.4 = (bf16[8,48,8,72]{3,2,1,0:T(8,128)(2,1)S(1)}, bf16[8,48,8,72]{3,2,1,0:T(8,128)(2,1)}, u32[]{:S(2)}) copy-start(bf16[8,48,8,72]{3,2,1,0:T(8,128)(2,1)} %reshape.268) | copy-start | bytes 1327108
  93.1 17.1 %copy-start.1 = (bf16[1,6,64,1152]{3,2,1,0:T(8,128)(2,1)S(1)}, bf16[1,6,64,1152]{3,2,1,0:T(8,128)(2,1)}, u32[]{:S(2)}) copy-start(bf16[1,6,64,1152]{3,2,1,0:T(8,128)(2,1)} %copy-done) | copy-start | bytes 2654212
where the time goes:
time: 114 us; the launch traced here: 113 us
  blocking collectives  75.5 us (66%)
  matrix products  22 us (19%)
  local copies, waits for them, and re-layouts  13.9 us (12%)
  other arithmetic  1.71 us (2%)
    all_to_all x1, blocking collectives, per_device(): lax.all_to_all(grouped, 'frame', split_axis=1, concat_axis=0, tiled=True)  28.1 us
    all_to_all x1, blocking collectives, per_device(): lax.all_to_all(latents, 'height', split_axis=2, concat_axis=1, tiled=True)  20.1 us
    all_to_all x1, blocking collectives, per_device(): lax.all_to_all(frames_att, 'frame', split_axis=0, concat_axis=1, tiled=True)  16.4 us
    all_to_all x1, blocking collectives, per_device(): lax.all_to_all(rows_att, 'height', split_axis=1, concat_axis=2, tiled=True)  10.9 us
    dot_general x2, matrix products, project(): joined = jnp.dot(flattened, weight, preferred_element_type=jnp.float32)  6.84 us
    dot_general x2, matrix products, residual(): jnp.dot(mixture.reshape(-1, mixture.shape[-1]), weight, preferred_element...  5.45 us
    sub x2, matrix products, attend(): scores = scores - jnp.max(scores, axis=-1, keepdims=True)  5.41 us
    dot_general x2, matrix products, attend(): jnp.einsum('bnlm,mbnd->lbnd', weights, value_rows, preferred_element_type...  4.31 us

commit v1 on v0

--- a/solution.py
+++ b/solution.py
@@ -4,6 +4,18 @@
 from jax.sharding import PartitionSpec as P
 
 HEAD_DIM = 72
+
+
+def in_blocks(x, dim, size):
+    shape = x.shape
+    tiles = x.reshape(*shape[:dim], size, shape[dim] // size, *shape[dim + 1 :])
+    return jnp.moveaxis(tiles, dim, 0)
+
+
+def laid_out(blocks, dim):
+    dims = list(blocks.shape[1:])
+    dims[dim] *= blocks.shape[0]
+    return jnp.moveaxis(blocks, 0, dim).reshape(dims)
 
 
 def layer_norm(values):
@@ -71,7 +83,15 @@
             lax.all_to_all(grouped, "frame", split_axis=1, concat_axis=0, tiled=True), qkv_weight[1]
         )
     )
-    frames_att = lax.all_to_all(frames_att, "frame", split_axis=0, concat_axis=1, tiled=True)
+    size, index = (lax.axis_size("frame"), lax.axis_index("frame"))
+    blocks = in_blocks(frames_att, 0, size)
+    out = blocks
+    for lap in range(1, size):
+        target, source = ((index + lap) % size, (index - lap) % size)
+        sent = lax.dynamic_index_in_dim(blocks, target, 0)
+        received = lax.ppermute(sent, "frame", [(i, (i + lap) % size) for i in range(size)])
+        out = lax.dynamic_update_slice_in_dim(out, received, source, axis=0)
+    frames_att = laid_out(out, 1)
     frames_att = frames_att.reshape(frames_dev, rows_dev, columns, frames_att.shape[-1])
     return residual(middle, frames_att, out_weight[1])
 

time: 114 us -> 112 us (0.982)
  blocking collectives: 75.5 us -> 31 us
  waiting for transfers between devices: 0 us -> 25.5 us
  starting transfers between devices: 0 us -> 15.7 us
    all_to_all x2 -> x0, blocking collectives: 44.5 us -> none  [the longest x1 28.1 us: per_device(): lax.all_to_all(grouped, 'frame', split_axis=1, concat_axis=0, tiled=True)]
    all_to_all x0 -> x1, waiting for transfers between devices: none -> 22.2 us  [per_device(): lax.all_to_all(grouped, 'frame', split_axis=1, concat_axis=0, tiled=True)]
    ppermute x0 -> x7, starting transfers between devices: none -> 9.83 us  [per_device(): lax.ppermute(sent, 'frame', [(i, (i + lap) % size) for i in range(size)])]
    all_to_all x0 -> x1, starting transfers between devices: none -> 5.82 us  [per_device(): lax.all_to_all(grouped, 'frame', split_axis=1, concat_axis=0, tiled=True)]
    ppermute x0 -> x7, waiting for transfers between devices: none -> 3.31 us  [per_device(): lax.ppermute(sent, 'frame', [(i, (i + lap) % size) for i in range(size)])]
  transfers between devices with their start and end apart: 0 -> 8, of which waited for: 0 -> 4; matrix products, arithmetic and copies ran while one was open for 0% -> 1% of each run, Pallas kernels for 0% -> 0%
where the time goes in v1:
time: 112 us
  blocking collectives  31 us (28%)
  waiting for transfers between devices  25.5 us (23%)
  matrix products  23.1 us (21%)
  starting transfers between devices  15.7 us (14%)
  local copies, waits for them, and re-layouts  14.6 us (13%)
  other arithmetic  1.72 us (2%)
    all_to_all x1, waiting for transfers between devices, per_device(): lax.all_to_all(grouped, 'frame', split_axis=1, concat_axis=0, tiled=True)  22.2 us
    all_to_all x1, blocking collectives, per_device(): lax.all_to_all(latents, 'height', split_axis=2, concat_axis=1, tiled=True)  20.1 us
    all_to_all x1, blocking collectives, per_device(): lax.all_to_all(rows_att, 'height', split_axis=1, concat_axis=2, tiled=True)  10.9 us
    ppermute x7, starting transfers between devices, per_device(): lax.ppermute(sent, 'frame', [(i, (i + lap) % size) for i in range(size)])  9.83 us
    dot_general x2, matrix products, project(): joined = jnp.dot(flattened, weight, preferred_element_type=jnp.float32)  6.85 us
    dot_general x2, matrix products, residual(): jnp.dot(mixture.reshape(-1, mixture.shape[-1]), weight, preferred_element...  6.59 us
    all_to_all x1, starting transfers between devices, per_device(): lax.all_to_all(grouped, 'frame', split_axis=1, concat_axis=0, tiled=True)  5.82 us
    sub x2, matrix products, attend(): scores = scores - jnp.max(scores, axis=-1, keepdims=True)  5.41 us
  transfers between devices with their start and end apart: 8, of which 4 were waited for; matrix products, arithmetic and copies ran while one was open for 1% of the time, Pallas kernels for 0%

profile of v1, /device:TPU:0, one launch (start us, length us, event | category | flops | bytes accessed | tf_op | source)
XLA Modules:
  0.0 111.9 jit_solution(4870966234256798093)
XLA Ops:
  0.0 1.7 %copy.35 = bf16[1,6,64,1152]{3,1,0,2:T(8,128)(2,1)S(1)} copy(bf16[1,6,64,1152]{3,2,1,0:T(8,128)(2,1)} %param.3) | data formatting | bytes 1769472 | tf_op args[0]
  1.7 20.1 %all_to_all.33 = bf16[1,6,64,1152]{3,1,0,2:T(8,128)(2,1)S(1)} all-to-all(bf16[1,6,64,1152]{3,1,0,2:T(8,128)(2,1)S(1)} %copy.35), channel_id=1, replica_groups=mesh['frame'=8,'height'=4] {'height'}, dimensions={2} | all-to-all | bytes 1769472 | tf_op jit(solution)/shard_map/all_to_all | solution.py:73
  22.9 2.4 %fusion.12 = bf16[384,1728]{0,1:T(8,128)(2,1)S(1)} fusion(bf16[384,1152]{1,0:T(8,128)(2,1)S(1)} %bitcast.111, bf16[2,1152,1728]{1,2,0:T(8,128)(2,1)S(1)} %copy-done.3), kind=kOutput, calls=%fused_computation.14 | convolution fusion | flops 1529487360 | bytes 6193152 | tf_op jit(solution)/shard_map/dot_general | solution.py:31
  25.3 1.8 %copy.38 = bf16[384,1728]{1,0:T(8,128)(2,1)S(1)} copy(bf16[384,1728]{0,1:T(8,128)(2,1)S(1)} %fusion.12) | data formatting | bytes 2654208 | tf_op jit(solution)/shard_map/convert_element_type | solution.py:32
  27.3 0.8 reshape.267
  28.1 0.8 reshape.268
  28.9 1.7 %reshape.266 = bf16[24,16,8,72]{3,2,1,0:T(8,128)(2,1)} reshape(bf16[1,24,16,576]{3,2,1,0:T(8,128)(2,1)S(1)} %get-tuple-element.8) | data formatting | bytes 884736 | tf_op jit(solution)/shard_map/reshape.7
  30.6 2.6 %fusion.69 = (f32[16,8,24]{2,1,0:T(8,128)S(1)}, f32[16,8,24,24]{2,3,1,0:T(8,128)}) fusion(bf16[24,16,8,72]{3,2,1,0:T(8,128)(2,1)S(1)} %reshape.268, bf16[24,16,8,72]{3,2,1,0:T(8,128)(2,1)S(1)} %reshape.267), kind=kOutput, calls=%fused_computation.79 | convolution fusion | flops 10838039 | bytes 1191936 | tf_op jit(solution)/shard_map/vmap()/sub | solution.py:47
  33.2 2.1 %fusion.37 = bf16[1,24,16,8,72]{4,1,3,2,0:T(8,128)(2,1)S(1)} fusion(f32[16,8,24,24]{2,3,1,0:T(8,128)} %get-tuple-element.19, bf16[24,16,8,72]{3,2,1,0:T(8,128)(2,1)S(1)} %copy-done.1, f32[16,8,24]{2,1,0:T(8,128)S(1)} %get-tuple-element.18), kind=kOutput, calls=%fused_computation.45 | convolution fusion | flops 10985472 | bytes 1191936 | tf_op jit(solution)/shard_map/vmap(bnlm,mbnd->lbnd)/dot_general | solution.py:50
  36.1 10.9 %all_to_all.34 = bf16[1,24,16,576]{3,2,0,1:T(8,128)(2,1)S(1)} all-to-all(bf16[1,24,16,576]{3,2,0,1:T(8,128)(2,1)S(1)} %bitcast.108), channel_id=1, replica_groups=mesh['frame'=8,'height'=4] {'height'}, dimensions={1} | all-to-all | bytes 884736 | tf_op jit(solution)/shard_map/all_to_all | solution.py:77
  47.0 3.2 %fusion.10 = bf16[1,6,64,1152]{3,2,1,0:T(8,128)(2,1)} fusion(bf16[6,64,576]{2,1,0:T(8,128)(2,1)S(1)} %bitcast.113, bf16[1,6,64,1152]{3,2,1,0:T(8,128)(2,1)S(1)} %copy-done, bf16[2,576,1152]{2,1,0:T(8,128)(2,1)} %param.5), kind=kOutput, calls=%fused_computation.12 | convolution fusion | flops 510935040 | bytes 3538944 | tf_op jit(solution)/shard_map/dot_general | solution.py:55
  50.2 5.8 %all-to-all-start.2 = ((bf16[1,8,48,1152]{3,2,0,1:T(8,128)(2,1)}), bf16[1,8,48,1152]{3,2,0,1:T(8,128)(2,1)S(1)}, u32[]{:S(2)}, u32[]{:S(2)}) async-start(bf16[1,8,48,1152]{3,2,0,1:T(8,128)(2,1)} %bitcast.16), calls=%async_computation.2 | async-start | bytes 1769472 | tf_op jit(solution)/shard_map/all_to_all | solution.py:83
  56.1 22.2 %all-to-all-done.2 = bf16[1,8,48,1152]{3,2,0,1:T(8,128)(2,1)S(1)} async-done(((bf16[1,8,48,1152]{3,2,0,1:T(8,128)(2,1)}), bf16[1,8,48,1152]{3,2,0,1:T(8,128)(2,1)S(1)}, u32[]{:S(2)}, u32[]{:S(2)}) %all-to-all-start.2) | async-done | bytes 884768 | tf_op jit(solution)/shard_map/all_to_all | solution.py:83
  79.2 4.5 %fusion.15 = bf16[384,1728]{0,1:T(8,128)(2,1)S(1)} fusion(bf16[384,1152]{1,0:T(8,128)(2,1)S(1)} %bitcast.110, bf16[2,1152,1728]{1,2,0:T(8,128)(2,1)} %param.4), kind=kOutput, calls=%fused_computation.15 | convolution fusion | flops 1529487360 | bytes 6193152 | tf_op jit(solution)/shard_map/dot_general | solution.py:31
  83.6 1.8 %copy.47 = bf16[384,1728]{1,0:T(8,128)(2,1)S(1)} copy(bf16[384,1728]{0,1:T(8,128)(2,1)S(1)} %fusion.15) | data formatting | bytes 2654208 | tf_op jit(solution)/shard_map/convert_element_type | solution.py:32
  85.7 0.8 reshape.272
  86.5 0.8 reshape.273
  87.3 1.7 %reshape.271 = bf16[8,48,8,72]{3,2,1,0:T(8,128)(2,1)} reshape(bf16[8,48,576]{2,1,0:T(8,128)(2,1)S(1)} %get-tuple-element.5) | data formatting | bytes 884736 | tf_op jit(solution)/shard_map/reshape | solution.py:43
  88.9 2.8 %fusion.74 = (f32[48,8,8]{2,1,0:T(8,128)S(1)}, f32[48,8,8,8]{2,3,1,0:T(8,128)}) fusion(bf16[8,48,8,72]{3,2,1,0:T(8,128)(2,1)S(1)} %reshape.273, bf16[8,48,8,72]{3,2,1,0:T(8,128)(2,1)S(1)} %reshape.272), kind=kOutput, calls=%fused_computation.80 | convolution fusion | flops 3612679 | bytes 995328 | tf_op jit(solution)/shard_map/sub | solution.py:47
  91.7 2.2 %fusion.38 = bf16[8,48,8,72]{3,0,2,1:T(8,128)(2,1)S(1)} fusion(f32[48,8,8,8]{2,3,1,0:T(8,128)} %get-tuple-element.21, bf16[8,48,8,72]{3,2,1,0:T(8,128)(2,1)S(1)} %copy-done.2, f32[48,8,8]{2,1,0:T(8,128)S(1)} %get-tuple-element.20), kind=kOutput, calls=%fused_computation.46 | convolution fusion | flops 3809280 | bytes 995328 | tf_op jit(solution)/shard_map/bnlm,mbnd->lbnd/dot_general | solution.py:50
  94.0 0.6 convert_element_type.152
  94.7 1.3 %collective-permute-start = (bf16[1,1,1,48,576]{4,3,0,2,1:T(8,128)(2,1)S(1)}, bf16[1,1,1,48,576]{4,3,0,2,1:T(8,128)(2,1)S(1)}, u32[]{:S(2)}, u32[]{:S(2)}) collective-permute-start(bf16[1,1,1,48,576]{4,3,0,2,1:T(8,128)(2,1)S(1)} %get-tuple-element.17), channel_id=1, source_target_pairs={{0,4},{4,8},{8,12},{12,16},{16,20},{20,24},{24,28},{28,0},{1,5},{5... | collective-permute-start | bytes 165896 | tf_op jit(solution)/shard_map/ppermute | solution.py:92
  95.9 0.6 convert_element_type.151
  96.6 1.7 %collective-permute-start.2 = (bf16[1,1,1,48,576]{4,3,0,2,1:T(8,128)(2,1)S(1)}, bf16[1,1,1,48,576]{4,3,0,2,1:T(8,128)(2,1)S(1)}, u32[]{:S(2)}, u32[]{:S(2)}) collective-permute-start(bf16[1,1,1,48,576]{4,3,0,2,1:T(8,128)(2,1)S(1)} %get-tuple-element.15), channel_id=1, source_target_pairs={{0,12},{4,16},{8,20},{12,24},{16,28},{20,0},{24,4},{28,8},{1,13},{... | collective-permute-start | bytes 165896 | tf_op jit(solution)/shard_map/ppermute | solution.py:92
  98.3 2.4 %collective-permute-start.3 = (bf16[1,1,1,48,576]{4,3,0,2,1:T(8,128)(2,1)S(1)}, bf16[1,1,1,48,576]{4,3,0,2,1:T(8,128)(2,1)S(1)}, u32[]{:S(2)}, u32[]{:S(2)}) collective-permute-start(bf16[1,1,1,48,576]{4,3,0,2,1:T(8,128)(2,1)S(1)} %get-tuple-element.14), channel_id=1, source_target_pairs={{0,16},{4,20},{8,24},{12,28},{16,0},{20,4},{24,8},{28,12},{1,17},{... | collective-permute-start | bytes 165896 | tf_op jit(solution)/shard_map/ppermute | solution.py:92
  100.7 1.7 %collective-permute-start.4 = (bf16[1,1,1,48,576]{4,3,0,2,1:T(8,128)(2,1)S(1)}, bf16[1,1,1,48,576]{4,3,0,2,1:T(8,128)(2,1)S(1)}, u32[]{:S(2)}, u32[]{:S(2)}) collective-permute-start(bf16[1,1,1,48,576]{4,3,0,2,1:T(8,128)(2,1)S(1)} %get-tuple-element.13), channel_id=1, source_target_pairs={{0,20},{4,24},{8,28},{12,0},{16,4},{20,8},{24,12},{28,16},{1,21},{... | collective-permute-start | bytes 165896 | tf_op jit(solution)/shard_map/ppermute | solution.py:92
  102.4 1.8 %collective-permute-start.5 = (bf16[1,1,1,48,576]{4,3,0,2,1:T(8,128)(2,1)S(1)}, bf16[1,1,1,48,576]{4,3,0,2,1:T(8,128)(2,1)S(1)}, u32[]{:S(2)}, u32[]{:S(2)}) collective-permute-start(bf16[1,1,1,48,576]{4,3,0,2,1:T(8,128)(2,1)S(1)} %get-tuple-element.12), channel_id=1, source_target_pairs={{0,24},{4,28},{8,0},{12,4},{16,8},{20,12},{24,16},{28,20},{1,25},{... | collective-permute-start | bytes 165896 | tf_op jit(solution)/shard_map/ppermute | solution.py:92
  104.2 0.9 collective-permute-start.6
  105.2 1.2 %collective-permute-done.3 = bf16[1,1,1,48,576]{4,3,0,2,1:T(8,128)(2,1)S(1)} collective-permute-done((bf16[1,1,1,48,576]{4,3,0,2,1:T(8,128)(2,1)S(1)}, bf16[1,1,1,48,576]{4,3,0,2,1:T(8,128)(2,1)S(1)}, u32[]{:S(2)}, u32[]{:S(2)}) %collective-permute-start.3) | collective-permute-done | bytes 55328 | tf_op jit(solution)/shard_map/ppermute | solution.py:92
  106.4 1.2 %collective-permute-done.4 = bf16[1,1,1,48,576]{4,3,0,2,1:T(8,128)(2,1)S(1)} collective-permute-done((bf16[1,1,1,48,576]{4,3,0,2,1:T(8,128)(2,1)S(1)}, bf16[1,1,1,48,576]{4,3,0,2,1:T(8,128)(2,1)S(1)}, u32[]{:S(2)}, u32[]{:S(2)}) %collective-permute-start.4) | collective-permute-done | bytes 55328 | tf_op jit(solution)/shard_map/ppermute | solution.py:92
  107.6 0.9 collective-permute-done.6
  108.5 3.4 %fusion.11 = bf16[1,6,64,1152]{3,2,1,0:T(8,128)(2,1)} fusion(bf16[6,64,576]{2,1,0:T(8,128)(2,1)S(1)} %bitcast.112, bf16[1,6,64,1152]{3,2,1,0:T(8,128)(2,1)} %fusion.10, bf16[2,576,1152]{2,1,0:T(8,128)(2,1)} %param.5), kind=kOutput, calls=%fused_computation.13 | convolution fusion | flops 510935040 | bytes 3538944 | tf_op jit(solution)/shard_map/dot_general | solution.py:55
  (39 shorter events, 3.6 us)
Async XLA Ops:
  1.7 21.2 %copy-start.3 = (bf16[2,1152,1728]{1,2,0:T(8,128)(2,1)S(1)}, bf16[2,1152,1728]{1,2,0:T(8,128)(2,1)}, u32[]{:S(2)}) copy-start(bf16[2,1152,1728]{1,2,0:T(8,128)(2,1)} %param.4) | copy-start | bytes 23887876
  30.6 2.6 %copy-start.1 = (bf16[24,16,8,72]{3,2,1,0:T(8,128)(2,1)S(1)}, bf16[24,16,8,72]{3,2,1,0:T(8,128)(2,1)}, u32[]{:S(2)}) copy-start(bf16[24,16,8,72]{3,2,1,0:T(8,128)(2,1)} %reshape.266) | copy-start | bytes 1327108
  35.5 11.5 %copy-start = (bf16[1,6,64,1152]{3,2,1,0:T(8,128)(2,1)S(1)}, bf16[1,6,64,1152]{3,2,1,0:T(8,128)(2,1)}, u32[]{:S(2)}) copy-start(bf16[1,6,64,1152]{3,2,1,0:T(8,128)(2,1)} %param.3) | copy-start | bytes 2654212
  50.2 28.0 %all-to-all-start.2 = ((bf16[1,8,48,1152]{3,2,0,1:T(8,128)(2,1)}), bf16[1,8,48,1152]{3,2,0,1:T(8,128)(2,1)S(1)}, u32[]{:S(2)}, u32[]{:S(2)}) async-start(bf16[1,8,48,1152]{3,2,0,1:T(8,128)(2,1)} %bitcast.16), calls=%async_computation.2 | async-start | bytes 1769472 | tf_op jit(solution)/shard_map/all_to_all | solution.py:83
  88.9 2.8 %copy-start.2 = (bf16[8,48,8,72]{3,2,1,0:T(8,128)(2,1)S(1)}, bf16[8,48,8,72]{3,2,1,0:T(8,128)(2,1)}, u32[]{:S(2)}) copy-start(bf16[8,48,8,72]{3,2,1,0:T(8,128)(2,1)} %reshape.271) | copy-start | bytes 1327108
  94.7 7.8 %collective-permute-start = (bf16[1,1,1,48,576]{4,3,0,2,1:T(8,128)(2,1)S(1)}, bf16[1,1,1,48,576]{4,3,0,2,1:T(8,128)(2,1)S(1)}, u32[]{:S(2)}, u32[]{:S(2)}) collective-permute-start(bf16[1,1,1,48,576]{4,3,0,2,1:T(8,128)(2,1)S(1)} %get-tuple-element.17), channel_id=1, source_target_pairs={{0,4},{4,8},{8,12},{12,16},{16,20},{20,24},{24,28},{28,0},{1,5},{5... | collective-permute-start | bytes 165896 | tf_op jit(solution)/shard_map/ppermute | solution.py:92
  96.5 7.7 %collective-permute-start.1 = (bf16[1,1,1,48,576]{4,3,0,2,1:T(8,128)(2,1)S(1)}, bf16[1,1,1,48,576]{4,3,0,2,1:T(8,128)(2,1)S(1)}, u32[]{:S(2)}, u32[]{:S(2)}) collective-permute-start(bf16[1,1,1,48,576]{4,3,0,2,1:T(8,128)(2,1)S(1)} %get-tuple-element.16), channel_id=1, source_target_pairs={{0,8},{4,12},{8,16},{12,20},{16,24},{20,28},{24,0},{28,4},{1,9},{5... | collective-permute-start | bytes 165896 | tf_op jit(solution)/shard_map/ppermute | solution.py:92
  96.6 8.5 %collective-permute-start.2 = (bf16[1,1,1,48,576]{4,3,0,2,1:T(8,128)(2,1)S(1)}, bf16[1,1,1,48,576]{4,3,0,2,1:T(8,128)(2,1)S(1)}, u32[]{:S(2)}, u32[]{:S(2)}) collective-permute-start(bf16[1,1,1,48,576]{4,3,0,2,1:T(8,128)(2,1)S(1)} %get-tuple-element.15), channel_id=1, source_target_pairs={{0,12},{4,16},{8,20},{12,24},{16,28},{20,0},{24,4},{28,8},{1,13},{... | collective-permute-start | bytes 165896 | tf_op jit(solution)/shard_map/ppermute | solution.py:92
  98.3 8.0 %collective-permute-start.3 = (bf16[1,1,1,48,576]{4,3,0,2,1:T(8,128)(2,1)S(1)}, bf16[1,1,1,48,576]{4,3,0,2,1:T(8,128)(2,1)S(1)}, u32[]{:S(2)}, u32[]{:S(2)}) collective-permute-start(bf16[1,1,1,48,576]{4,3,0,2,1:T(8,128)(2,1)S(1)} %get-tuple-element.14), channel_id=1, source_target_pairs={{0,16},{4,20},{8,24},{12,28},{16,0},{20,4},{24,8},{28,12},{1,17},{... | collective-permute-start | bytes 165896 | tf_op jit(solution)/shard_map/ppermute | solution.py:92
  100.7 6.9 %collective-permute-start.4 = (bf16[1,1,1,48,576]{4,3,0,2,1:T(8,128)(2,1)S(1)}, bf16[1,1,1,48,576]{4,3,0,2,1:T(8,128)(2,1)S(1)}, u32[]{:S(2)}, u32[]{:S(2)}) collective-permute-start(bf16[1,1,1,48,576]{4,3,0,2,1:T(8,128)(2,1)S(1)} %get-tuple-element.13), channel_id=1, source_target_pairs={{0,20},{4,24},{8,28},{12,0},{16,4},{20,8},{24,12},{28,16},{1,21},{... | collective-permute-start | bytes 165896 | tf_op jit(solution)/shard_map/ppermute | solution.py:92
  102.4 5.2 %collective-permute-start.5 = (bf16[1,1,1,48,576]{4,3,0,2,1:T(8,128)(2,1)S(1)}, bf16[1,1,1,48,576]{4,3,0,2,1:T(8,128)(2,1)S(1)}, u32[]{:S(2)}, u32[]{:S(2)}) collective-permute-start(bf16[1,1,1,48,576]{4,3,0,2,1:T(8,128)(2,1)S(1)} %get-tuple-element.12), channel_id=1, source_target_pairs={{0,24},{4,28},{8,0},{12,4},{16,8},{20,12},{24,16},{28,20},{1,25},{... | collective-permute-start | bytes 165896 | tf_op jit(solution)/shard_map/ppermute | solution.py:92
  104.2 4.3 %collective-permute-start.6 = (bf16[1,1,1,48,576]{4,3,0,2,1:T(8,128)(2,1)S(1)}, bf16[1,1,1,48,576]{4,3,0,2,1:T(8,128)(2,1)S(1)}, u32[]{:S(2)}, u32[]{:S(2)}) collective-permute-start(bf16[1,1,1,48,576]{4,3,0,2,1:T(8,128)(2,1)S(1)} %get-tuple-element.11), channel_id=1, source_target_pairs={{0,28},{4,0},{8,4},{12,8},{16,12},{20,16},{24,20},{28,24},{1,29},{... | collective-permute-start | bytes 165896 | tf_op jit(solution)/shard_map/ppermute | solution.py:92
